TPU v7x, 256 devices: a whole 4x4x8 slice. The times are simulated.
256 devices in a mesh: band: 4 (over x_hi, core), grid: 64 (over x_lo, z, y).
Axes of the slice: x: 4 (x_hi: 2, x_lo: 2; x = x_hi * 2 + x_lo), y: 4, z: 8, core: 2. Of those that a mesh axis runs over, the one named last changes fastest.
Arguments:
- orbitals: float32 [768, 16, 16, 512], P('grid', None, None, 'band'), may hold values from -24 to 24
- potential: float32 [768, 16, 16], P('grid'), may hold values from -3 to -1
- projectors: float32 [256, 8, 13, 256], P('grid'), may hold values from -0.109375 to 0.109375
- atom_planes: int32 [256, 13], P('grid'), may hold values from 0 to 23, as said below
- kb_energy: float32 [8], replicated, may hold values from 1 to 4
Outputs:
- filtered: float32 [768, 16, 16, 512], P('grid', None, None, 'band')
- correlation_gram: float32 [512, 512], P('band')
Inputs may be any that keep to these rules, and one draw needn't show every extreme that they name: `atom_planes`: each atom's row holds 13 consecutive plane numbers; the first atom starts at plane 0 and the last atom at plane 12 - 1.
All inputs are finite; a program needn't handle non-finite values.
Results may differ from a plain program's by a relative error of at most 0.0003.
Values sent between devices are 32-bit elements; how exact they have to be, the bound alone decides.
A program may use at most 128 MiB of HBM per device.

v0:
```python
import jax
import jax.numpy as jnp
from jax import lax
from jax.sharding import PartitionSpec as P

DEGREE = 4


WEIGHTS = (
    -5369.0 / 1800.0,
    12.0 / 7.0,
    -15.0 / 56.0,
    10.0 / 189.0,
    -1.0 / 112.0,
    2.0 / 1925.0,
    -1.0 / 16632.0,
)
LOWER = -4.0
CUTOFF = 1.0
UPPER = 16.0
PRECISE = lax.Precision.HIGHEST


def padded(array, sides, width):
    for axis, dim in sides:
        peers, length = (lax.axis_size(axis), array.shape[dim])
        up = [(i, (i + 1) % peers) for i in range(peers)]
        down = [(j, i) for i, j in up]
        last = lax.slice_in_dim(array, length - width, length, axis=dim)
        initial = lax.slice_in_dim(array, 0, width, axis=dim)
        before = lax.ppermute(last, axis, up)
        after = lax.ppermute(initial, axis, down)
        array = jnp.concatenate([before, array, after], axis=dim)
    return array


def shifted(array, axis, by):
    peers = lax.axis_size(axis)
    return lax.ppermute(array, axis, [(i, (i + by) % peers) for i in range(peers)])


def filter_terms(degree):
    half_span = (UPPER - CUTOFF) / 2.0
    middle = (UPPER + CUTOFF) / 2.0
    sigma_now = half_span / (LOWER - middle)
    sigma_first = sigma_now
    scales = [sigma_now / half_span]
    recall = [0.0]
    for level in range(1, degree):
        sigma_next = 1.0 / (2.0 / sigma_first - sigma_now)
        scales.append(2.0 * sigma_next / half_span)
        recall.append(sigma_now * sigma_next)
        sigma_now = sigma_next
    return (middle, scales, recall)


def second_roll(values, along):
    summed = WEIGHTS[0] * values
    for reach in range(1, 7):
        summed = summed + WEIGHTS[reach] * (
            jnp.roll(values, reach, along) + jnp.roll(values, -reach, along)
        )
    return summed


def second_planes(widened, slab_planes):
    summed = WEIGHTS[0] * widened[6 : 6 + slab_planes]
    for reach in range(1, 7):
        summed = summed + WEIGHTS[reach] * (
            widened[6 + reach : 6 + reach + slab_planes]
            + widened[6 - reach : 6 - reach + slab_planes]
        )
    return summed


def shards(orbitals, potential, projectors, atom_planes, kb_energy):
    slab_planes = orbitals.shape[0]
    orb_here = orbitals.shape[-1]
    extent = slab_planes + 12
    atom_count = atom_planes.shape[0]
    plane_marks = (
        atom_planes[:, :, None] == jnp.arange(extent, dtype=jnp.int32)[None, None, :]
    ).astype(jnp.float32)
    projector_map = jnp.einsum("abe,apbs->apes", plane_marks, projectors, precision=PRECISE)
    map_rows = atom_count * projectors.shape[1]
    projector_map = projector_map.reshape(map_rows, -1)
    energy_col = jnp.tile(kb_energy, atom_count)[:, None]
    middle, scales, recall = filter_terms(DEGREE)
    previous = orbitals
    current = orbitals
    for level in range(DEGREE):
        widened = padded(current, (("grid", 0),), 6)
        lap = (
            second_planes(widened, slab_planes) + second_roll(current, 1) + second_roll(current, 2)
        )
        local_part = -0.5 * lap + potential[..., None] * current
        correlation = (
            jnp.dot(projector_map, widened.reshape(-1, orb_here), precision=PRECISE) * energy_col
        )
        spread = lax.dot_general(
            projector_map, correlation, (((0,), (0,)), ((), ())), precision=PRECISE
        )
        spread = spread.reshape(widened.shape)
        own_part = local_part + spread[6 : 6 + slab_planes]
        low_rim = spread[:6]
        high_rim = spread[6 + slab_planes :]
        from_below = shifted(high_rim, "grid", 1)
        from_above = shifted(low_rim, "grid", -1)
        applied = own_part.at[:6].add(from_below).at[slab_planes - 6 :].add(from_above)
        result = scales[level] * (applied - middle * current)
        if level > 0:
            result = result - recall[level] * previous
        previous = current
        current = result
    flattened = current.reshape(-1, orb_here)
    piece = lax.all_gather(current, "band", axis=3, tiled=True)
    gram_part = lax.dot_general(
        flattened, piece.reshape(-1, piece.shape[-1]), (((0,), (0,)), ((), ())), precision=PRECISE
    )
    gram_total = lax.psum(gram_part, "grid")
    cell_count = slab_planes * orbitals.shape[1] * orbitals.shape[2] * lax.axis_size("grid")
    correlation_gram = gram_total * (1.0 / cell_count)
    return (current, correlation_gram)


def solution(mesh):
    return jax.shard_map(
        shards,
        mesh=mesh,
        in_specs=(
            P("grid", None, None, "band"),
            P("grid", None, None),
            P("grid", None, None, None),
            P("grid", None),
            P(),
        ),
        out_specs=(P("grid", None, None, "band"), P("band", None)),
        check_vma=False,
    )
```

profile of v0, /device:TPU:4, one launch (start us, length us, event | category | flops | bytes accessed | tf_op | source)
XLA Modules:
  0.0 995.4 jit_solution(16665948579629088824)
XLA Ops:
  7.2 2.8 fusion.325
  11.6 7.4 collective-permute-start
  47.2 2.0 fusion.309
  60.2 5.1 fusion.326
  70.2 6.2 collective-permute-start.3
  77.7 14.2 %fusion.105 = f32[12,16,16,128]{3,2,1,0:T(8,128)S(1)} fusion(f32[12,16,16,128]{3,2,1,0:T(8,128)S(1)} %bitcast.60, f32[18,16,16,128]{3,2,1,0:T(8,128)S(1)} %get-tuple-element.305, f32[18,16,16,128]{3,2,1,0:T(8,128)S(1)} %constant_dynamic-update-slice_fusion, f32[12,15,16,128]{3,2,1,0:T(8,128)} %get-tuple-element.301, ...), kind=kLoop, calls=%fused_computation.176 | loop fusion | flops 33423360 | bytes 61353984 | tf_op jit(solution)/shard_map/add | solution.py:104
  118.3 2.1 fusion.282
  122.4 2.1 fusion.284
  124.5 2.1 fusion.280
  126.6 6.4 collective-permute-start.4
  137.7 11.2 %collective-permute-done.5 = f32[6,16,16,128]{3,2,1,0:T(8,128)S(1)} collective-permute-done((f32[6,16,16,128]{3,2,1,0:T(8,128)S(1)}, f32[6,16,16,128]{3,2,1,0:T(8,128)S(1)}, u32[]{:S(2)}, u32[]{:S(2)}) %collective-permute-start.5) | collective-permute-done | bytes 786464 | tf_op jit(solution)/shard_map/ppermute | solution.py:31
  151.6 5.1 fusion.327
  159.2 6.6 collective-permute-start.7
  165.8 20.1 %fusion.71 = f32[12,16,16,128]{3,2,1,0:T(8,128)} fusion(f32[12,16,16,128]{3,2,1,0:T(8,128)} %bitcast.61, f32[12,16,16,128]{3,2,1,0:T(8,128)S(1)} %broadcast_multiply_fusion, f32[6,16,16,128]{3,2,1,0:T(8,128)S(1)} %collective-permute-done.5, f32[6,16,16,128]{3,2,1,0:T(8,128)} %copy-done.9, f32[12,15,16,128]{3,2,1,0:T(8,128)} %get-tuple-element.251, ...), kind=kLoop, calls=%fused_computation.135 | loop fusion | flops 38928384 | bytes 47198208 | tf_op jit(solution)/shard_map/add | solution.py:104
  185.9 2.4 fusion.215
  188.2 2.4 fusion.214
  222.0 6.4 collective-permute-start.8
  233.1 9.9 collective-permute-done.9
  245.6 5.1 fusion.328
  252.1 6.4 collective-permute-start.11
  258.6 19.8 %fusion.40 = f32[12,16,16,128]{3,2,1,0:T(8,128)} fusion(f32[12,16,16,128]{3,2,1,0:T(8,128)S(1)} %bitcast.62, f32[12,16,16,128]{3,2,1,0:T(8,128)S(1)} %multiply_subtract_fusion.2, f32[6,16,16,128]{3,2,1,0:T(8,128)S(1)} %collective-permute-done.9, f32[6,16,16,128]{3,2,1,0:T(8,128)} %copy-done.11, f32[12,15,16,128]{3,2,1,0:T(8,128)} %get-tuple-element.201, ...), kind=kLoop, calls=%fused_computation.104 | loop fusion | flops 38141952 | bytes 44052480 | tf_op jit(solution)/shard_map/add | solution.py:104
  278.4 2.3 fusion.213
  280.7 2.4 fusion.212
  283.1 2.0 multiply_subtract_fusion.1
  315.2 6.6 collective-permute-start.12
  326.6 8.2 collective-permute-done.13
  337.4 5.1 fusion.329
  343.9 6.5 collective-permute-start.15
  350.4 18.8 %fusion.9 = f32[12,16,16,128]{3,2,1,0:T(8,128)S(1)} fusion(f32[12,16,16,128]{3,2,1,0:T(8,128)S(1)} %bitcast.63, f32[12,16,16,128]{3,2,1,0:T(8,128)S(1)} %multiply_subtract_fusion.1, f32[6,16,16,128]{3,2,1,0:T(8,128)S(1)} %collective-permute-done.13, f32[6,16,16,128]{3,2,1,0:T(8,128)} %copy-done.10, f32[12,15,16,128]{3,2,1,0:T(8,128)} %get-tuple-element.151, ...), kind=kLoop, calls=%fused_computation.73 | loop fusion | flops 38141952 | bytes 44052480 | tf_op jit(solution)/shard_map/add | solution.py:104
  373.4 45.7 %all-gather.2.cloned.1.call-done = f32[12,16,16,512]{3,2,1,0:T(8,128)} async-done(((f32[12,16,16,128]{3,2,1,0:T(8,128)}), f32[12,16,16,512]{3,2,1,0:T(8,128)}) %all-gather.2.cloned.1.call-update) | async-done | bytes 6291472 | tf_op jit(solution)/shard_map/all_gather | solution.py:116
  419.2 7.4 convolution_bitcast_fusion.1
  426.6 560.1 %all-reduce.2.cloned.1.call-done = f32[128,512]{1,0:T(8,128)} async-done(((f32[128,512]{1,0:T(8,128)}), f32[128,512]{1,0:T(8,128)}) %all-reduce.2.cloned.1.call-update) | async-done | bytes 262160 | tf_op jit(solution)/shard_map/psum | solution.py:120
  (187 shorter events, 170.0 us)
Async XLA Ops:
  7.2 42.1 %copy-start = (f32[4,8,13,256]{3,1,2,0:T(8,128)S(1)}, f32[4,8,13,256]{3,1,2,0:T(8,128)}, u32[]{:S(2)}) copy-start(f32[4,8,13,256]{3,1,2,0:T(8,128)} %param.23) | copy-start | bytes 1277956
  7.2 11.8 %copy-start.2 = (f32[12,16,16,128]{3,2,1,0:T(8,128)S(1)}, f32[12,16,16,128]{3,2,1,0:T(8,128)}, u32[]{:S(2)}) copy-start(f32[12,16,16,128]{3,2,1,0:T(8,128)} %param.21) | copy-start | bytes 4718596
  7.2 412.0 %all-gather.2.cloned.1.call-start = ((), (), s32[]{:S(2)}) async-start(), calls=%async_computation | async-start | bytes 7864320 | tf_op jit(solution)/shard_map/all_gather | solution.py:116
  10.0 46.8 %collective-permute-start.1 = (f32[6,16,16,128]{3,2,1,0:T(8,128)}, f32[6,16,16,128]{3,2,1,0:T(8,128)}, u32[]{:S(2)}, u32[]{:S(2)}) collective-permute-start(f32[6,16,16,128]{3,2,1,0:T(8,128)} %get-tuple-element.306), channel_id=1, source_target_pairs={{0,1},{1,2},{2,3},{3,4},{4,5},{5,6},{6,7},{7,8},{8,9},{9,10},{10,1... | collective-permute-start | bytes 2359304 | tf_op jit(solution)/shard_map/ppermute | solution.py:31
  11.6 45.2 %collective-permute-start = (f32[6,16,16,128]{3,2,1,0:T(8,128)}, f32[6,16,16,128]{3,2,1,0:T(8,128)}, u32[]{:S(2)}, u32[]{:S(2)}) collective-permute-start(f32[6,16,16,128]{3,2,1,0:T(8,128)} %get-tuple-element.307), channel_id=1, source_target_pairs={{1,0},{2,1},{3,2},{4,3},{5,4},{6,5},{7,6},{8,7},{9,8},{10,9},{11,1... | collective-permute-start | bytes 2359304 | tf_op jit(solution)/shard_map/ppermute | solution.py:32
  47.2 2.1 copy-start.15
  47.2 3.6 copy-start.14
  47.2 4.2 copy-start.16
  68.3 9.3 copy-start.12
  68.3 9.3 copy-start.13
  69.6 8.1 copy-start.5
  69.6 8.1 copy-start.6
  69.6 8.1 copy-start.7
  70.1 7.6 slice-start
  70.1 23.6 %collective-permute-start.2 = (f32[6,16,16,128]{3,2,1,0:T(8,128)}, f32[6,16,16,128]{3,2,1,0:T(8,128)}, u32[]{:S(2)}, u32[]{:S(2)}) collective-permute-start(f32[6,16,16,128]{3,2,1,0:T(8,128)} %bitcast.5), channel_id=1, source_target_pairs={{0,1},{1,2},{2,3},{3,4},{4,5},{5,6},{6,7},{7,8},{8,9},{9,10},{10,1... | collective-permute-start | bytes 2359304 | tf_op jit(solution)/shard_map/ppermute | solution.py:39
  70.2 24.9 %collective-permute-start.3 = (f32[6,16,16,128]{3,2,1,0:T(8,128)}, f32[6,16,16,128]{3,2,1,0:T(8,128)}, u32[]{:S(2)}, u32[]{:S(2)}) collective-permute-start(f32[6,16,16,128]{3,2,1,0:T(8,128)} %bitcast.6), channel_id=1, source_target_pairs={{0,63},{1,0},{2,1},{3,2},{4,3},{5,4},{6,5},{7,6},{8,7},{9,8},{10,9... | collective-permute-start | bytes 2359304 | tf_op jit(solution)/shard_map/ppermute | solution.py:39
  126.6 22.4 %collective-permute-start.5 = (f32[6,16,16,128]{3,2,1,0:T(8,128)S(1)}, f32[6,16,16,128]{3,2,1,0:T(8,128)S(1)}, u32[]{:S(2)}, u32[]{:S(2)}) collective-permute-start(f32[6,16,16,128]{3,2,1,0:T(8,128)S(1)} %get-tuple-element.254), channel_id=1, source_target_pairs={{0,1},{1,2},{2,3},{3,4},{4,5},{5,6},{6,7},{7,8},{8,9},{9,10},{10,1... | collective-permute-start | bytes 2359304 | tf_op jit(solution)/shard_map/ppermute | solution.py:31
  126.6 22.4 %collective-permute-start.4 = (f32[6,16,16,128]{3,2,1,0:T(8,128)S(1)}, f32[6,16,16,128]{3,2,1,0:T(8,128)S(1)}, u32[]{:S(2)}, u32[]{:S(2)}) collective-permute-start(f32[6,16,16,128]{3,2,1,0:T(8,128)S(1)} %get-tuple-element.255), channel_id=1, source_target_pairs={{1,0},{2,1},{3,2},{4,3},{5,4},{6,5},{7,6},{8,7},{9,8},{10,9},{11,1... | collective-permute-start | bytes 2359304 | tf_op jit(solution)/shard_map/ppermute | solution.py:32
  159.2 26.7 %collective-permute-start.6 = (f32[6,16,16,128]{3,2,1,0:T(8,128)}, f32[6,16,16,128]{3,2,1,0:T(8,128)}, u32[]{:S(2)}, u32[]{:S(2)}) collective-permute-start(f32[6,16,16,128]{3,2,1,0:T(8,128)} %bitcast.9), channel_id=1, source_target_pairs={{0,1},{1,2},{2,3},{3,4},{4,5},{5,6},{6,7},{7,8},{8,9},{9,10},{10,1... | collective-permute-start | bytes 2359304 | tf_op jit(solution)/shard_map/ppermute | solution.py:39
  159.2 29.1 %collective-permute-start.7 = (f32[6,16,16,128]{3,2,1,0:T(8,128)}, f32[6,16,16,128]{3,2,1,0:T(8,128)}, u32[]{:S(2)}, u32[]{:S(2)}) collective-permute-start(f32[6,16,16,128]{3,2,1,0:T(8,128)} %bitcast.10), channel_id=1, source_target_pairs={{0,63},{1,0},{2,1},{3,2},{4,3},{5,4},{6,5},{7,6},{8,7},{9,8},{10,9... | collective-permute-start | bytes 2359304 | tf_op jit(solution)/shard_map/ppermute | solution.py:39
  222.0 20.9 %collective-permute-start.9 = (f32[6,16,16,128]{3,2,1,0:T(8,128)S(1)}, f32[6,16,16,128]{3,2,1,0:T(8,128)S(1)}, u32[]{:S(2)}, u32[]{:S(2)}) collective-permute-start(f32[6,16,16,128]{3,2,1,0:T(8,128)S(1)} %get-tuple-element.204), channel_id=1, source_target_pairs={{0,1},{1,2},{2,3},{3,4},{4,5},{5,6},{6,7},{7,8},{8,9},{9,10},{10,1... | collective-permute-start | bytes 2359304 | tf_op jit(solution)/shard_map/ppermute | solution.py:31
  222.0 20.9 %collective-permute-start.8 = (f32[6,16,16,128]{3,2,1,0:T(8,128)S(1)}, f32[6,16,16,128]{3,2,1,0:T(8,128)S(1)}, u32[]{:S(2)}, u32[]{:S(2)}) collective-permute-start(f32[6,16,16,128]{3,2,1,0:T(8,128)S(1)} %get-tuple-element.205), channel_id=1, source_target_pairs={{1,0},{2,1},{3,2},{4,3},{5,4},{6,5},{7,6},{8,7},{9,8},{10,9},{11,1... | collective-permute-start | bytes 2359304 | tf_op jit(solution)/shard_map/ppermute | solution.py:32
  252.1 26.2 %collective-permute-start.10 = (f32[6,16,16,128]{3,2,1,0:T(8,128)}, f32[6,16,16,128]{3,2,1,0:T(8,128)}, u32[]{:S(2)}, u32[]{:S(2)}) collective-permute-start(f32[6,16,16,128]{3,2,1,0:T(8,128)} %bitcast.13), channel_id=1, source_target_pairs={{0,1},{1,2},{2,3},{3,4},{4,5},{5,6},{6,7},{7,8},{8,9},{9,10},{10,1... | collective-permute-start | bytes 2359304 | tf_op jit(solution)/shard_map/ppermute | solution.py:39
  252.1 28.6 %collective-permute-start.11 = (f32[6,16,16,128]{3,2,1,0:T(8,128)}, f32[6,16,16,128]{3,2,1,0:T(8,128)}, u32[]{:S(2)}, u32[]{:S(2)}) collective-permute-start(f32[6,16,16,128]{3,2,1,0:T(8,128)} %bitcast.14), channel_id=1, source_target_pairs={{0,63},{1,0},{2,1},{3,2},{4,3},{5,4},{6,5},{7,6},{8,7},{9,8},{10,9... | collective-permute-start | bytes 2359304 | tf_op jit(solution)/shard_map/ppermute | solution.py:39
  315.2 19.5 %collective-permute-start.13 = (f32[6,16,16,128]{3,2,1,0:T(8,128)S(1)}, f32[6,16,16,128]{3,2,1,0:T(8,128)S(1)}, u32[]{:S(2)}, u32[]{:S(2)}) collective-permute-start(f32[6,16,16,128]{3,2,1,0:T(8,128)S(1)} %get-tuple-element.154), channel_id=1, source_target_pairs={{0,1},{1,2},{2,3},{3,4},{4,5},{5,6},{6,7},{7,8},{8,9},{9,10},{10,1... | collective-permute-start | bytes 2359304 | tf_op jit(solution)/shard_map/ppermute | solution.py:31
  315.2 19.5 %collective-permute-start.12 = (f32[6,16,16,128]{3,2,1,0:T(8,128)S(1)}, f32[6,16,16,128]{3,2,1,0:T(8,128)S(1)}, u32[]{:S(2)}, u32[]{:S(2)}) collective-permute-start(f32[6,16,16,128]{3,2,1,0:T(8,128)S(1)} %get-tuple-element.155), channel_id=1, source_target_pairs={{1,0},{2,1},{3,2},{4,3},{5,4},{6,5},{7,6},{8,7},{9,8},{10,9},{11,1... | collective-permute-start | bytes 2359304 | tf_op jit(solution)/shard_map/ppermute | solution.py:32
  342.6 7.7 copy-start.8
  343.9 25.3 %collective-permute-start.14 = (f32[6,16,16,128]{3,2,1,0:T(8,128)}, f32[6,16,16,128]{3,2,1,0:T(8,128)}, u32[]{:S(2)}, u32[]{:S(2)}) collective-permute-start(f32[6,16,16,128]{3,2,1,0:T(8,128)} %bitcast.17), channel_id=1, source_target_pairs={{0,1},{1,2},{2,3},{3,4},{4,5},{5,6},{6,7},{7,8},{8,9},{9,10},{10,1... | collective-permute-start | bytes 2359304 | tf_op jit(solution)/shard_map/ppermute | solution.py:39
  343.9 26.7 %collective-permute-start.15 = (f32[6,16,16,128]{3,2,1,0:T(8,128)}, f32[6,16,16,128]{3,2,1,0:T(8,128)}, u32[]{:S(2)}, u32[]{:S(2)}) collective-permute-start(f32[6,16,16,128]{3,2,1,0:T(8,128)} %bitcast.18), channel_id=1, source_target_pairs={{0,63},{1,0},{2,1},{3,2},{4,3},{5,4},{6,5},{7,6},{8,7},{9,8},{10,9... | collective-permute-start | bytes 2359304 | tf_op jit(solution)/shard_map/ppermute | solution.py:39
  373.4 45.8 %copy-start.3 = (f32[12,16,16,128]{3,2,1,0:T(8,128)S(1)}, f32[12,16,16,128]{3,2,1,0:T(8,128)}, u32[]{:S(2)}) copy-start(f32[12,16,16,128]{3,2,1,0:T(8,128)} %multiply_subtract_fusion) | copy-start | bytes 4718596
  373.4 613.3 %all-reduce.2.cloned.1.call-start = ((), (), s32[]{:S(2)}) async-start(), calls=%async_computation.1 | async-start | bytes 524288 | tf_op jit(solution)/shard_map/psum | solution.py:120
  419.2 569.2 %copy-start.1 = (f32[4,8,13,256]{3,1,2,0:T(8,128)S(1)}, f32[4,8,13,256]{3,1,2,0:T(8,128)}, u32[]{:S(2)}) copy-start(f32[4,8,13,256]{3,1,2,0:T(8,128)} %param.23) | copy-start | bytes 1277956
  (4 other events, 4.5 us)
Sparse Core Ops, SparseCore 0:
  373.5 45.6 all-gather.1
  426.7 559.9 all-reduce.1
where the time goes:
time: 1010 us; the launch traced here: 995 us
  waiting for transfers between devices  637 us (63%)
  local copies, waits for them, and re-layouts  155 us (15%)
  other arithmetic  98.3 us (10%)
  starting transfers between devices  54.4 us (5%)
  matrix products  36.1 us (4%)
  between operations  14.6 us (1%)
    psum x1, waiting for transfers between devices, shards(): gram_total = lax.psum(gram_part, 'grid')  560 us
    slice x96, local copies, waits for them, and re-layouts, second_roll(): jnp.roll(values, -reach, along)  137 us
    add x4, other arithmetic, shards(): own_part = local_part + spread[6:6 + slab_planes]  72.9 us
    all_gather x1, waiting for transfers between devices, shards(): piece = lax.all_gather(current, 'band', axis=3, tiled=True)  45.7 us
    ppermute x4, waiting for transfers between devices, padded(): before = lax.ppermute(last, axis, up)  29.3 us
    ppermute x4, starting transfers between devices, padded(): after = lax.ppermute(initial, axis, down)  26.8 us
    ppermute x8, starting transfers between devices, shifted(): lax.ppermute(array, axis, [(i, (i + by) % peers) for i in range(peers)])  25.9 us
    dot_general x4, matrix products, shards(): lax.dot_general(projector_map, correlation, (((0,), (0,)), ((), ())), pre...  20.3 us
  transfers between devices with their start and end apart: 18, of which 6 were waited for; matrix products, arithmetic and copies ran while one was open for 13% of the time, Pallas kernels for 0%

commit v1 on v0

v1 whole, which is shorter than its diff:
```python
import functools

import jax
import jax.numpy as jnp
import ml_dtypes
import numpy as np
from jax import lax
from jax.experimental import pallas as pl
from jax.experimental.pallas import tpu as pltpu
from jax.sharding import PartitionSpec as P

DEGREE = 4
WEIGHTS = (
    -5369.0 / 1800.0,
    12.0 / 7.0,
    -15.0 / 56.0,
    10.0 / 189.0,
    -1.0 / 112.0,
    2.0 / 1925.0,
    -1.0 / 16632.0,
)
LOWER = -4.0
CUTOFF = 1.0
UPPER = 16.0
REACH = 6
CHUNKS = 4
YPEERS = 4
MESH = pl.DeviceIdType.MESH
F32 = jnp.float32
BF16 = jnp.bfloat16


def filter_terms(degree):
    half_span = (UPPER - CUTOFF) / 2.0
    middle = (UPPER + CUTOFF) / 2.0
    sigma_now = half_span / (LOWER - middle)
    sigma_first = sigma_now
    scales = [sigma_now / half_span]
    recall = [0.0]
    for level in range(1, degree):
        sigma_next = 1.0 / (2.0 / sigma_first - sigma_now)
        scales.append(2.0 * sigma_next / half_span)
        recall.append(sigma_now * sigma_next)
        sigma_now = sigma_next
    return (middle, scales, recall)


def plane_matrix(ny, nz):
    cells = ny * nz
    matrix = np.zeros((cells, cells))
    for y in range(ny):
        for z in range(nz):
            for reach in range(1, REACH + 1):
                for by in (reach, -reach):
                    matrix[y * nz + z, ((y + by) % ny) * nz + z] += -0.5 * WEIGHTS[reach]
                    matrix[y * nz + z, y * nz + (z + by) % nz] += -0.5 * WEIGHTS[reach]
    high = matrix.astype(ml_dtypes.bfloat16)
    low = (matrix - high.astype(np.float64)).astype(ml_dtypes.bfloat16)
    return np.concatenate([high, low], axis=0)


def split(value):
    high = value.astype(BF16)
    return high, (value - high.astype(F32)).astype(BF16)


def dot(a, b):
    return jnp.dot(a, b, preferred_element_type=F32)


def place_body(planes, projectors, placed):
    placed[...] = jnp.zeros_like(placed)
    atoms, count, blocks, _ = projectors.shape
    for atom in range(atoms):
        for block in range(blocks):
            placed[planes[atom, block], pl.ds(atom * count, count), :] = projectors[atom, :, block, :]


def main_body(
    cells,
    orb, pot_t, wyz, pown, energy,
    filt, gram,
    ys, halo_lo, halo_hi, diag, local, rim_lo, rim_hi, pstack, qstack,
    cpart, crecv, cown, cnear,
    fb, fc, fd, gacc, xsend, xrecv, gblk, ry, b1, rz, g1, gfull,
    hs, hr, rs_, rr_, ps_, pr_, cs_, cr_, fs_, fr_, xs_, xr_, ys_, yr_, zs_, zr_, as_, ar_, bs_, br_,
):
    slab, rows = orb.shape[0], orb.shape[1]
    step_rows = rows // CHUNKS
    band = lax.axis_index("band")
    grid = lax.axis_index("grid")
    domains = lax.axis_size("grid")
    right = lax.rem(grid + 1, domains)
    left = lax.rem(grid + domains - 1, domains)
    x_hi = band // 2
    partner = band + 1 - 2 * lax.rem(band, 2)
    opposite = lax.rem(band + 2, 4)
    diagonal = lax.rem(partner + 2, 4)
    y_here = lax.rem(grid, YPEERS)
    y_base = grid - y_here
    zx_here = grid // YPEERS
    zx_count = domains // YPEERS
    part_rows = b1.shape[0] // zx_count
    y_peers = [lax.rem(y_here + i, YPEERS) for i in range(1, YPEERS)]
    zx_peers = [lax.rem(zx_here + i, zx_count) for i in range(1, zx_count)]
    middle, scales, recall = filter_terms(DEGREE)
    pending = []

    def remote(src, dst, ssem, rsem, b, g):
        return pltpu.make_async_remote_copy(
            src_ref=src, dst_ref=dst, send_sem=ssem, recv_sem=rsem,
            device_id=(b, g), device_id_type=MESH,
        )

    def start(*copies):
        for copy in copies:
            copy.start()
            pending.append(copy)
        return copies

    barrier = pltpu.get_barrier_semaphore()
    greeted = [(band, left), (band, right), (partner, grid), (opposite, grid), (diagonal, grid)]
    greeted += [(band, y_base + q) for q in y_peers]
    greeted += [(band, m * YPEERS + y_here) for m in zx_peers]
    for b, g in greeted:
        pl.semaphore_signal(barrier, inc=1, device_id=(b, g), device_id_type=MESH)
    for p in range(slab):
        diag[p] = jnp.broadcast_to(
            pot_t[:, p : p + 1] + (-1.5 * WEIGHTS[0] - middle), (rows, orb.shape[2])
        )
    pl.semaphore_wait(barrier, len(greeted))

    def source(level):
        return orb if level == 0 else ys.at[level - 1]

    def halo(level, r):
        cur = source(level)
        at = pl.ds(r * step_rows, step_rows)
        return (
            remote(cur.at[pl.ds(slab - REACH, REACH), at], halo_lo.at[level, :, at],
                   hs.at[level, r, 0], hr.at[level, r, 0], band, right),
            remote(cur.at[pl.ds(0, REACH), at], halo_hi.at[level, :, at],
                   hs.at[level, r, 1], hr.at[level, r, 1], band, left),
        )

    extent = pown.shape[0]
    rims = start(
        remote(pown.at[pl.ds(extent - REACH, REACH)], rim_lo, rs_.at[0], rr_.at[0], band, right),
        remote(pown.at[pl.ds(0, REACH)], rim_hi, rs_.at[1], rr_.at[1], band, left),
    )
    sent = {}
    for r in range(2):
        sent[0, r] = start(*halo(0, r))
    for copy in rims:
        copy.wait_recv()

    def stack_map(low):
        def step(p, carry):
            rim = rim_lo[p] if low else rim_hi[p]
            at = p if low else p + REACH
            both = jnp.concatenate([pown[at + REACH], rim], axis=0)
            high, rest = split(both)
            pstack[at] = jnp.concatenate([high, rest], axis=0)
            high = high.astype(F32)
            rest = both - high
            turned = jnp.concatenate([high, high, rest, jnp.zeros_like(rest)], axis=0)
            qstack[at] = jnp.transpose(turned).astype(BF16)
            return carry
        lax.fori_loop(0, REACH, step, 0)

    stack_map(True)
    stack_map(False)

    def plane_products(cur, first):
        def step(p, total):
            high, rest = split(cur[p])
            pair = jnp.concatenate([high, rest], axis=1)
            lanes = high.shape[1]
            o = dot(wyz[...], pair)
            local[p] = o[:rows, :lanes] + o[:rows, lanes:] + o[rows:, :lanes]
            q = dot(pstack[p], pair)
            half = q.shape[0] // 2
            return total + (q[:half, :lanes] + q[:half, lanes:] + q[half:, :lanes])
        return lax.fori_loop(
            first, first + REACH, step, jnp.zeros((pstack.shape[1] // 2, orb.shape[2]), F32)
        )

    def spread_on(first, coeff):
        high = coeff.astype(BF16).astype(F32)
        rest = coeff - high
        stacked = jnp.concatenate([high, rest, high, jnp.zeros_like(rest)], axis=0).astype(BF16)

        def step(p, carry):
            local[p] = local[p] + dot(qstack[p], stacked)
            return carry
        lax.fori_loop(first, first + REACH, step, 0)

    def finish(level, r, target, copies):
        for copy in copies:
            copy.wait_recv()
        cur = source(level)
        prev = None if level == 0 else source(level - 1)
        scale = scales[level]
        taps = [-0.5 * scale * w for w in WEIGHTS]

        def step(i, carry):
            at = pl.ds(pl.multiple_of(r * step_rows + i * 8, 8), 8)
            line = [halo_lo[level, j, at] for j in range(REACH)]
            line += [cur[j, at] for j in range(slab)]
            line += [halo_hi[level, j, at] for j in range(REACH)]
            for j in range(slab):
                here = j + REACH
                value = scale * (local[j, at] + diag[j, at] * line[here])
                for reach in range(1, REACH + 1):
                    value = value + taps[reach] * (line[here - reach] + line[here + reach])
                if prev is not None:
                    value = value - recall[level] * prev[j, at]
                target[j, at] = value
            return carry
        lax.fori_loop(0, step_rows // 8, step, 0)

    width = energy.shape[0]
    shared = []
    for level in range(DEGREE):
        cur = source(level)
        low = plane_products(cur, 0)
        high = plane_products(cur, REACH)
        cpart[level, 0] = low[width:]
        cpart[level, 1] = high[width:]
        parts = start(
            remote(cpart.at[level, 1], crecv.at[level, 0], ps_.at[level, 0], pr_.at[level, 0], band, right),
            remote(cpart.at[level, 0], crecv.at[level, 1], ps_.at[level, 1], pr_.at[level, 1], band, left),
        )
        sent[level, 2] = start(*halo(level, 2))
        for copy in parts:
            copy.wait_recv()
        own = (low[:width] + high[:width] + crecv[level, 0] + crecv[level, 1]) * energy[...]
        cown[level] = own
        nears = start(
            remote(cown.at[level], cnear.at[level, 0], cs_.at[level, 0], cr_.at[level, 0], band, right),
            remote(cown.at[level], cnear.at[level, 1], cs_.at[level, 1], cr_.at[level, 1], band, left),
        )
        sent[level, 3] = start(*halo(level, 3))
        for copy in nears:
            copy.wait_recv()
        spread_on(0, jnp.concatenate([own, cnear[level, 0]], axis=0))
        spread_on(REACH, jnp.concatenate([own, cnear[level, 1]], axis=0))
        last = level == DEGREE - 1
        target = filt if last else ys.at[level]
        for r in range(CHUNKS):
            finish(level, r, target, sent[level, r])
            at = pl.ds(r * step_rows, step_rows)
            if not last:
                if r < 2:
                    sent[level + 1, r] = start(*halo(level + 1, r))
                continue
            shared.append(start(
                remote(filt.at[pl.ds(REACH * (1 - x_hi), REACH), at], fc.at[:, at],
                       fs_.at[r, 0], fr_.at[r, 0], opposite, grid),
                remote(filt.at[:, at], fb.at[:, at], fs_.at[r, 1], fr_.at[r, 1], partner, grid),
            ))

    forwarded = []
    for r in range(CHUNKS):
        at = pl.ds(r * step_rows, step_rows)
        shared[r][0].wait_recv()
        forwarded += start(
            remote(fc.at[:, at], fd.at[:, at], fs_.at[r, 2], fr_.at[r, 2], partner, grid)
        )
        shared[r][1].wait_recv()

    def gram_step(mine, other):
        a_high, a_rest = split(jnp.transpose(mine))
        b_high, b_rest = split(other)
        both = jnp.concatenate([a_high, a_rest], axis=0)
        first = dot(both, b_high)
        lanes = a_high.shape[0]
        return first[:lanes] + first[lanes:] + dot(a_high, b_rest)

    gacc[...] = jnp.zeros_like(gacc)

    def own_step(p, carry):
        mine = filt[p]
        gacc[0] = gacc[0] + gram_step(mine, jnp.concatenate([mine, fb[p]], axis=1))
        return carry
    lax.fori_loop(0, slab, own_step, 0)
    for copy in forwarded:
        copy.wait_recv()

    def cross_step(p, carry):
        mine = filt[p + REACH * x_hi]
        gacc[1] = gacc[1] + gram_step(mine, jnp.concatenate([fc[p], fd[p]], axis=1))
        return carry
    lax.fori_loop(0, REACH, cross_step, 0)

    lanes = orb.shape[2]
    xsend[0] = jnp.transpose(gacc[1, :, :lanes])
    xsend[1] = jnp.transpose(gacc[1, :, lanes:])
    crossed = start(
        remote(xsend.at[0], xrecv.at[0], xs_.at[0], xr_.at[0], opposite, grid),
        remote(xsend.at[1], xrecv.at[1], xs_.at[1], xr_.at[1], diagonal, grid),
    )
    gblk[0] = gacc[0, :, :lanes]
    gblk[1] = gacc[0, :, lanes:]
    for copy in crossed:
        copy.wait_recv()
    gblk[2] = gacc[1, :, :lanes] + xrecv[0]
    gblk[3] = gacc[1, :, lanes:] + xrecv[1]

    for i, q in enumerate(y_peers):
        start(remote(gblk.at[q], ry.at[y_here], ys_.at[i], yr_.at[y_here], band, y_base + q))
    total = gblk[y_here]
    for i, q in enumerate(y_peers):
        remote(ry.at[q], ry.at[q], ys_.at[i], yr_.at[q], band, y_base + q).wait_recv()
        total = total + ry[q]
    b1[...] = total

    def piece(ref, n):
        return ref.at[pl.ds(pl.multiple_of(n * part_rows, 8), part_rows)]

    for i, m in enumerate(zx_peers):
        start(remote(piece(b1, m), rz.at[zx_here], zs_.at[i], zr_.at[zx_here],
                     band, m * YPEERS + y_here))
    total = b1[pl.ds(pl.multiple_of(zx_here * part_rows, 8), part_rows)]
    for i, m in enumerate(zx_peers):
        remote(rz.at[m], rz.at[m], zs_.at[i], zr_.at[m], band, m * YPEERS + y_here).wait_recv()
        total = total + rz[m]
    g1[pl.ds(pl.multiple_of(zx_here * part_rows, 8), part_rows)] = total * (1.0 / cells)
    for i, m in enumerate(zx_peers):
        start(remote(piece(g1, zx_here), piece(g1, zx_here), as_.at[i], ar_.at[zx_here],
                     band, m * YPEERS + y_here))
    for i, m in enumerate(zx_peers):
        remote(piece(g1, m), piece(g1, m), as_.at[i], ar_.at[m],
               band, m * YPEERS + y_here).wait_recv()
    for i, q in enumerate(y_peers):
        start(remote(g1, gfull.at[y_here], bs_.at[i], br_.at[y_here], band, y_base + q))
    gfull[y_here] = g1[...]
    for i, q in enumerate(y_peers):
        remote(gfull.at[q], gfull.at[q], bs_.at[i], br_.at[q], band, y_base + q).wait_recv()
    for c in range(4):
        block = 2 * lax.rem(x_hi + c // 2, 2) + lax.rem(lax.rem(band, 2) + c % 2, 2)
        gram[:, c * lanes : (c + 1) * lanes] = gfull[block]
    for copy in pending:
        copy.wait_send()


def shards(orbitals, potential, projectors, atom_planes, kb_energy):
    slab, ny, nz, lanes = orbitals.shape
    rows = ny * nz
    domains = lax.axis_size("grid")
    atoms, count, blocks, _ = projectors.shape
    width = atoms * count
    extent = slab + 2 * REACH
    vmem = pl.BlockSpec(memory_space=pltpu.VMEM)
    placed = pl.pallas_call(
        place_body,
        out_shape=jax.ShapeDtypeStruct((extent, width, rows), F32),
        in_specs=[pl.BlockSpec(memory_space=pltpu.SMEM), vmem],
        out_specs=vmem,
        name="place_projectors",
    )(atom_planes, projectors)
    energy = jnp.broadcast_to(jnp.tile(kb_energy, atoms)[:, None], (width, lanes))
    pot_t = jnp.transpose(potential.reshape(slab, rows))
    zx_count = domains // YPEERS
    dma = pltpu.SemaphoreType.DMA
    big = (slab, rows, lanes)
    rim = (REACH, rows, lanes)
    small = (width, lanes)
    square = (lanes, lanes)
    scratch = [
        pltpu.VMEM((DEGREE - 1, *big), F32),
        pltpu.VMEM((DEGREE, *rim), F32),
        pltpu.VMEM((DEGREE, *rim), F32),
        pltpu.VMEM(big, F32),
        pltpu.VMEM(big, F32),
        pltpu.VMEM((REACH, width, rows), F32),
        pltpu.VMEM((REACH, width, rows), F32),
        pltpu.VMEM((slab, 4 * width, rows), BF16),
        pltpu.VMEM((slab, rows, 8 * width), BF16),
        pltpu.VMEM((DEGREE, 2, *small), F32),
        pltpu.VMEM((DEGREE, 2, *small), F32),
        pltpu.VMEM((DEGREE, *small), F32),
        pltpu.VMEM((DEGREE, 2, *small), F32),
        pltpu.VMEM(big, F32),
        pltpu.VMEM(rim, F32),
        pltpu.VMEM(rim, F32),
        pltpu.VMEM((2, lanes, 2 * lanes), F32),
        pltpu.VMEM((2, *square), F32),
        pltpu.VMEM((2, *square), F32),
        pltpu.VMEM((4, *square), F32),
        pltpu.VMEM((YPEERS, *square), F32),
        pltpu.VMEM(square, F32),
        pltpu.VMEM((zx_count, lanes // zx_count, lanes), F32),
        pltpu.VMEM(square, F32),
        pltpu.VMEM((YPEERS, *square), F32),
        dma((DEGREE, CHUNKS, 2)), dma((DEGREE, CHUNKS, 2)),
        dma((2,)), dma((2,)),
        dma((DEGREE, 2)), dma((DEGREE, 2)),
        dma((DEGREE, 2)), dma((DEGREE, 2)),
        dma((CHUNKS, 3)), dma((CHUNKS, 3)),
        dma((2,)), dma((2,)),
        dma((YPEERS,)), dma((YPEERS,)),
        dma((zx_count,)), dma((zx_count,)),
        dma((zx_count,)), dma((zx_count,)),
        dma((YPEERS,)), dma((YPEERS,)),
    ]
    filtered, gram = pl.pallas_call(
        functools.partial(main_body, slab * rows * domains),
        out_shape=(
            jax.ShapeDtypeStruct(big, F32),
            jax.ShapeDtypeStruct((lanes, 4 * lanes), F32),
        ),
        in_specs=[vmem] * 5,
        out_specs=(vmem, vmem),
        scratch_shapes=scratch,
        compiler_params=pltpu.CompilerParams(
            collective_id=0, has_side_effects=True, vmem_limit_bytes=56 << 20
        ),
        name="filter_and_gram",
    )(orbitals.reshape(big), pot_t, jnp.asarray(plane_matrix(ny, nz)), placed, energy)
    return (filtered.reshape(orbitals.shape), gram)


def solution(mesh):
    return jax.shard_map(
        shards,
        mesh=mesh,
        in_specs=(
            P("grid", None, None, "band"),
            P("grid", None, None),
            P("grid", None, None, None),
            P("grid", None),
            P(),
        ),
        out_specs=(P("grid", None, None, "band"), P("band", None)),
        check_vma=False,
    )
```

time: 1010 us -> 154 us (0.15); the launches traced: 995 us -> 153 us
  waiting for transfers between devices: 637 us -> 0 us
  local copies, waits for them, and re-layouts: 155 us -> 8.46 us
  Pallas kernels: 0 us -> 144 us
  other arithmetic: 98.3 us -> 0 us
  starting transfers between devices: 54.4 us -> 0 us
  matrix products: 36.1 us -> 0 us
  between operations: 14.6 us -> 0.65 us
    psum x1 -> x0, waiting for transfers between devices: 560 us -> none  [shards(): gram_total = lax.psum(gram_part, 'grid')]
    slice x109 -> x0, local copies, waits for them, and re-layouts: 147 us -> none  [the longest x96 137 us: second_roll(): jnp.roll(values, -reach, along)]
    pallas_call x0 -> x2, Pallas kernels: none -> 144 us  [the longest x1 142 us: shards(): pl.pallas_call(functools.partial(main_body, slab * rows * domains), out_s...]
    add x4 -> x0, other arithmetic: 72.9 us -> none  [shards(): own_part = local_part + spread[6:6 + slab_planes]]
    ppermute x16 -> x0, starting transfers between devices: 54.3 us -> none  [the longest x4 26.8 us: padded(): after = lax.ppermute(initial, axis, down)]
    all_gather x1 -> x0, waiting for transfers between devices: 45.7 us -> none  [shards(): piece = lax.all_gather(current, 'band', axis=3, tiled=True)]
    dot_general x10 -> x0, matrix products: 36.1 us -> none  [the longest x4 20.3 us: shards(): lax.dot_general(projector_map, correlation, (((0,), (0,)), ((), ())), pre...]
    ppermute x16 -> x0, waiting for transfers between devices: 31.1 us -> none  [the longest x4 29.3 us: padded(): before = lax.ppermute(last, axis, up)]
  transfers between devices with their start and end apart: 18 -> 0, of which waited for: 6 -> 0; matrix products, arithmetic and copies ran while one was open for 13% -> 0% of each run, Pallas kernels for 0% -> 0%
where the time goes in v1:
time: 154 us; the launch traced here: 153 us
  Pallas kernels  144 us (94%)
  local copies, waits for them, and re-layouts  8.46 us (5%)
    pallas_call x1, Pallas kernels, shards(): pl.pallas_call(functools.partial(main_body, slab * rows * domains), out_s...  142 us
    unnamed x6, local copies, waits for them, and re-layouts  7.04 us

profile of v1, /device:TPU:4, one launch (start us, length us, event | category | flops | bytes accessed | tf_op | source)
XLA Modules:
  0.0 153.1 jit_solution(16042427334144306152)
XLA Ops:
  0.6 0.7 tile.2
  1.3 0.1 broadcast_in_dim.7
  1.4 0.7 broadcast_in_dim.8.energy
  2.0 1.7 %copy.8 = f32[12,16,16]{0,2,1:T(8,128)} copy(f32[12,16,16]{2,1,0:T(8,128)} %param.7) | data formatting | bytes 24576 | tf_op args[1]
  3.8 1.9 %copy.9.projectors = f32[4,8,13,256]{3,2,1,0:T(8,128)} copy(f32[4,8,13,256]{3,1,2,0:T(8,128)} %param.8) | data formatting | bytes 851968 | tf_op args[2]
  5.7 2.1 %place_projectors.1.pown = f32[24,32,256]{2,1,0:T(8,128)} custom-call(s32[4,13]{1,0:T(4,128)} %planes.1, f32[4,8,13,256]{3,2,1,0:T(8,128)} %copy.9.projectors), custom_call_target="tpu_custom_call" | custom-call | tf_op jit(solution)/shard_map/place_projectors/pallas_call | solution.py:355
  7.8 141.9 %filter_and_gram.1 = (f32[12,256,128]{2,1,0:T(8,128)}, f32[128,512]{1,0:T(8,128)}) custom-call(f32[12,256,128]{2,1,0:T(8,128)} %bitcast.6, f32[256,12]{1,0:T(8,128)} %bitcast.7, bf16[512,256]{1,0:T(8,128)(2,1)} %constant.2.clone.wyz, f32[24,32,256]{2,1,0:T(8,128)} %place_projectors.1.pown, f32[32,128]{1,0:T(8,128)} %broadcast_in_dim.8.energy), custom_call_target="tpu_custom_call" | custom-call | tf_op jit(solution)/shard_map/filter_and_gram/pallas_call | solution.py:407
  149.7 0.0 copy-start
  149.7 2.7 %copy.12 = f32[12,16,16,128]{3,2,1,0:T(8,128)} copy(f32[12,16,16,128]{3,2,1,0:T(8,128)} %bitcast.5) | data formatting | bytes 3145728
  152.4 0.0 copy-done
  152.4 0.7 copy.13
Async XLA Ops:
  149.7 2.7 %copy-start = (f32[128,512]{1,0:T(8,128)S(1)}, f32[128,512]{1,0:T(8,128)}, u32[]{:S(2)}) copy-start(f32[128,512]{1,0:T(8,128)} %get-tuple-element.9) | copy-start | bytes 786436
